TPU v7x, 256 devices: a whole 4x4x8 slice. The times are simulated.
256 devices in a mesh: elec: 4 (over z_hi, core), row: 16 (over z_lo, y), col: 4 (over x).
Axes of the slice: x: 4, y: 4, z: 8 (z_hi: 2, z_lo: 4; z = z_hi * 4 + z_lo), core: 2. Of those that a mesh axis runs over, the one named last changes fastest.
Arguments:
- fields: bfloat16 [256, 2, 512, 256], P(('elec', 'row', 'col')), may hold values from -6 to 6
- mirror_phase: float32 [512, 256], replicated, may hold values from -3.140625 to 3.140625
- tile_list: int32 [16, 4, 9, 2], P('row', 'col'), may hold values from -1 to 31, as said below
Outputs:
- csd_tiles: float32 [16, 4, 9, 2, 768, 768], P('row', 'col', None, None, 'elec')
Inputs may be any that keep to these rules, and one draw needn't show every extreme that they name: `tile_list`: each slot of row index r and col index c holds a tile (i, j) of the lower triangle, j <= i, with i equal to r or 31 - r and j congruent to c modulo the number of col indices; every such tile appears in exactly one slot of its r and c, in drawn order; the other slots hold -1 in both entries.
All inputs are finite; a program needn't handle non-finite values.
Results may differ from a plain program's by a relative error of at most 0.012.
Values may be sent and summed in bfloat16 or wider, within the bound.
No kernel may reach another device: no remote copies, remote signals or barrier semaphores. Data moves between devices by JAX's collectives and lax.ppermute only.
A program may use at most 192 MiB of HBM per device.

v0:
```python
import math
import jax
import jax.numpy as jnp
from jax import lax
from jax.sharding import PartitionSpec as P

TILE = 768


def laid_out(pieces, dim):
    shape = list(pieces.shape[1:])
    shape[dim] *= pieces.shape[0]
    return jnp.moveaxis(pieces, 0, dim).reshape(shape)


def copy_for_each(x, axis):
    length = lax.axis_size(axis)
    return lax.all_to_all(jnp.broadcast_to(x[None], (length, *x.shape)), axis, 0, 0, tiled=True)


def gathered_copies(x, axis, dim):
    return laid_out(copy_for_each(x, axis), dim)


def dft_parts(length, sign_value):
    positions = jnp.arange(length, dtype=jnp.int32)
    product = positions[:, None] * positions[None, :] % length
    angles = 2.0 * math.pi / length * product.astype(jnp.float32)
    factor = 1.0 / math.sqrt(length)
    return (jnp.cos(angles) * factor, sign_value * jnp.sin(angles) * factor)


def left_table(length, sign_value, row_limit):
    real_part, imag_part = dft_parts(length, sign_value)
    real_part = real_part[:row_limit]
    imag_part = imag_part[:row_limit]
    return jnp.stack(
        [jnp.stack([real_part, -imag_part]), jnp.stack([imag_part, real_part])]
    ).astype(jnp.bfloat16)


def right_table(length, sign_value):
    real_part, imag_part = dft_parts(length, sign_value)
    return jnp.stack(
        [jnp.stack([real_part, imag_part]), jnp.stack([-imag_part, real_part])]
    ).astype(jnp.bfloat16)


def contract(formula, left_side, right_side):
    return jnp.einsum(formula, left_side, right_side, preferred_element_type=jnp.float32)


def propagate(fields, mirror_phase, slab_rows):
    length_x = fields.shape[2]
    length_y = fields.shape[3]
    cos_phase = jnp.cos(mirror_phase)
    sin_phase = jnp.sin(mirror_phase)
    first_pass = contract("dcwx,ecxy->edwy", left_table(length_x, -1.0, length_x), fields).astype(
        jnp.bfloat16
    )
    turned = contract("ecxy,cdyz->edxz", first_pass, right_table(length_y, -1.0))
    spectrum = jnp.stack(
        [
            turned[:, 0] * cos_phase - turned[:, 1] * sin_phase,
            turned[:, 0] * sin_phase + turned[:, 1] * cos_phase,
        ],
        axis=1,
    ).astype(jnp.bfloat16)
    back_rows = contract("dcwx,ecxy->edwy", left_table(length_x, 1.0, slab_rows), spectrum).astype(
        jnp.bfloat16
    )
    slab_part = contract("ecxy,cdyz->edxz", back_rows, right_table(length_y, 1.0)).astype(
        jnp.bfloat16
    )
    return slab_part.reshape(fields.shape[0], 2, slab_rows * length_y)


def accumulate(totals, row_part, col_part, row_labels, col_labels):
    row_real = row_part[..., 0, :, :]
    row_imag = row_part[..., 1, :, :]
    col_real = col_part[..., 0, :, :]
    col_imag = col_part[..., 1, :, :]
    formula = row_labels + "sp," + col_labels + "mq->smqp"
    real_sum = contract(formula, row_real, col_real) + contract(formula, row_imag, col_imag)
    imag_sum = contract(formula, row_imag, col_real) - contract(formula, row_real, col_imag)
    return totals + jnp.stack([real_sum, imag_sum], axis=2)


def body(fields, mirror_phase, tile_list):
    electrons = fields.shape[0]
    row_devices = lax.axis_size("row")
    col_devices = lax.axis_size("col")
    elec_devices = lax.axis_size("elec")
    tile_count = 2 * row_devices
    quarter = TILE // elec_devices
    window = tile_count * TILE
    spread = tile_count // col_devices
    group_size = elec_devices * col_devices
    total_electrons = electrons * elec_devices * row_devices * col_devices
    slab_field = propagate(fields, mirror_phase, window // fields.shape[3])
    entries = tile_list[0, 0]
    tile_row = entries[:, 0]
    tile_col = entries[:, 1]
    upper_pick = (tile_row >= row_devices).astype(jnp.int32)
    column = jnp.maximum(tile_col, 0) // col_devices
    is_listed = tile_row >= 0
    zero_carry = jnp.zeros((2, spread, 2, quarter, TILE), jnp.float32)
    blocks = slab_field.reshape(electrons, 2, tile_count, TILE)
    lower_tiles = blocks[:, :, :row_devices]
    higher_tiles = jnp.flip(blocks[:, :, row_devices:], axis=2)
    row_send = jnp.transpose(jnp.stack([lower_tiles, higher_tiles], axis=3), (2, 0, 1, 3, 4))
    row_mine = lax.all_to_all(row_send, "row", split_axis=0, concat_axis=1, tiled=True)
    col_send = blocks.reshape(electrons, 2, spread, col_devices, elec_devices, quarter)
    col_send = jnp.transpose(col_send, (4, 3, 0, 1, 2, 5)).reshape(
        group_size, electrons, 2, spread * quarter
    )
    col_mine = lax.all_to_all(col_send, ("elec", "col"), split_axis=0, concat_axis=1, tiled=True)
    row_panel = lax.all_gather(row_mine, ("elec", "col"), axis=0, tiled=True)
    row_panel = row_panel.reshape(group_size, row_devices, electrons, 2, 2, TILE)
    shard_piece = gathered_copies(col_mine, "row", 0)
    piece_rows = shard_piece.shape[0]
    col_part = shard_piece.reshape(piece_rows, group_size, electrons, 2, spread, quarter)
    totals = accumulate(zero_carry, row_panel, col_part, "abe", "bae")
    flat_blocks = totals.reshape(2 * spread, 2, quarter, TILE)
    result = jnp.take(flat_blocks, upper_pick * spread + column, axis=0)
    result = jnp.where(is_listed[:, None, None, None], result, jnp.zeros_like(result))
    result = result * (1.0 / math.sqrt(total_electrons))
    return result[None, None]


def solution(mesh):
    in_specs = (P(("elec", "row", "col"), None, None, None), P(), P("row", "col", None, None))
    out_specs = P("row", "col", None, None, "elec", None)
    return jax.shard_map(body, mesh=mesh, in_specs=in_specs, out_specs=out_specs, check_vma=False)
```

profile of v0, /device:TPU:1, one launch (start us, length us, event | category | flops | bytes accessed | tf_op | source)
XLA Modules:
  0.0 209.4 jit_solution(8675355788218229331)
XLA Ops:
  6.5 1.0 negate_convert_fusion.1
  7.5 1.7 multiply_convert_fusion.1
  9.3 1.7 multiply_convert_fusion.3
  10.9 4.4 %negate_convert_fusion = (bf16[1,512,512]{2,1,0:T(8,128)(2,1)S(1)}, bf16[1,512,512]{2,1,0:T(8,128)(2,1)S(1)}) fusion(), kind=kLoop, calls=%fused_computation.41 | loop fusion | flops 4980736 | bytes 1048576 | tf_op jit(solution)/shard_map/convert.21
  15.3 4.0 %fusion.35 = bf16[1,512,512]{2,1,0:T(8,128)(2,1)S(1)} fusion(), kind=kLoop, calls=%fused_computation.48 | loop fusion | flops 4194304 | bytes 524288 | tf_op jit(solution)/shard_map/convert.17
  19.3 1.5 fusion.28
  20.8 2.1 copy.37
  22.9 2.8 %fusion.79 = (f32[512,256]{0,1:T(8,128)S(1)}, f32[512,256]{0,1:T(8,128)S(1)}) fusion(f32[512,256]{0,1:T(8,128)} %copy.37), kind=kLoop, calls=%fused_computation.118 | loop fusion | bytes 1572864 | tf_op jit(solution)/shard_map/sin | solution.py:57
  25.7 2.4 %fusion.72 = (bf16[1,96,512]{2,1,0:T(8,128)(2,1)}, bf16[1,96,512]{2,1,0:T(8,128)(2,1)}, bf16[1,96,512]{2,1,0:T(8,128)(2,1)}) fusion(f32[512,512]{1,0:T(8,128)} %fusion.28), kind=kLoop, calls=%fused_computation.104 | loop fusion | flops 294912 | bytes 491520 | tf_op jit(solution)/shard_map/stack | solution.py:38
  28.0 1.5 maximum_bitcast_fusion
  29.5 2.0 fusion.59
  31.6 0.0 copy-done
  31.6 3.2 %convolution_bitcast_fusion = f32[1,2,512,256]{2,3,1,0:T(8,128)S(1)} fusion(bf16[1,2,512,512]{3,2,1,0:T(8,128)(2,1)} %get-tuple-element.17, bf16[1,2,512,512]{3,2,1,0:T(8,128)(2,1)} %get-tuple-element.16, bf16[1,2,256,256]{2,3,0,1:T(8,128)(2,1)} %get-tuple-element.19, bf16[1,2,256,256]{2,3,0,1:T(8,128)(2,1)} %get-tuple-element.18, ...), kind=kOutput, calls=%fused_computation.20 | convolution fusion | flops 806879232 | bytes 4194304 | tf_op jit(solution)/shard_map/ecxy,cdyz->edxz/dot_general | solution.py:50
  34.8 0.3 fusion.63
  35.0 0.0 copy-done.5
  35.0 0.0 copy-done.6
  35.1 0.0 copy-done.7
  35.1 1.7 fusion.22
  36.8 0.1 reshape_reshape_reshape.3
  37.0 0.1 reshape.301
  37.2 0.7 copy.42
  37.9 12.4 %all-to-all-start = ((bf16[16,1,2,1536]{3,2,1,0:T(2,128)(2,1)}), bf16[16,1,2,1536]{3,2,1,0:T(2,128)(2,1)S(1)}, u32[]{:S(2)}, u32[]{:S(2)}) async-start(bf16[16,1,2,1536]{3,2,1,0:T(2,128)(2,1)} %copy.42), calls=%async_computation | async-start | bytes 196608 | tf_op jit(solution)/shard_map/all_to_all | solution.py:117
  50.3 0.1 reshape_reshape.7
  50.5 0.8 maximum_bitcast_fusion.7
  51.3 8.8 %all-to-all-done = bf16[16,1,2,1536]{3,2,1,0:T(2,128)(2,1)S(1)} async-done(((bf16[16,1,2,1536]{3,2,1,0:T(2,128)(2,1)}), bf16[16,1,2,1536]{3,2,1,0:T(2,128)(2,1)S(1)}, u32[]{:S(2)}, u32[]{:S(2)}) %all-to-all-start) | async-done | bytes 98336 | tf_op jit(solution)/shard_map/all_to_all | solution.py:117
  60.1 6.0 %all-to-all-start.2 = ((bf16[16,1,2,2,768]{4,2,3,1,0:T(2,128)(2,1)}), bf16[16,1,2,2,768]{4,2,3,1,0:T(2,128)(2,1)S(1)}, u32[]{:S(2)}, u32[]{:S(2)}) async-start(bf16[16,1,2,2,768]{4,2,3,1,0:T(2,128)(2,1)} %maximum_bitcast_fusion.7), calls=%async_computation.2 | async-start | bytes 196608 | tf_op jit(solution)/shard_map/all_to_all | solution.py:112
  66.2 7.5 %all-to-all-done.2 = bf16[16,1,2,2,768]{4,2,3,1,0:T(2,128)(2,1)S(1)} async-done(((bf16[16,1,2,2,768]{4,2,3,1,0:T(2,128)(2,1)}), bf16[16,1,2,2,768]{4,2,3,1,0:T(2,128)(2,1)S(1)}, u32[]{:S(2)}, u32[]{:S(2)}) %all-to-all-start.2) | async-done | bytes 98336 | tf_op jit(solution)/shard_map/all_to_all | solution.py:112
  73.7 1.3 broadcast_in_dim.24
  75.0 4.4 %all-to-all-start.1 = ((bf16[16,1,16,2,1536]{4,2,3,1,0:T(8,128)(2,1)}), bf16[16,1,16,2,1536]{4,2,3,1,0:T(8,128)(2,1)}, u32[]{:S(2)}, u32[]{:S(2)}) async-start(bf16[16,1,16,2,1536]{4,2,3,1,0:T(8,128)(2,1)} %broadcast_in_dim.24), calls=%async_computation.1 | async-start | bytes 3145728 | tf_op jit(solution)/shard_map/all_to_all | solution.py:18
  79.4 0.0 all-gather.3.cloned.1.call-start
  79.5 0.7 copy.47
  80.2 0.0 all-gather.3.cloned.1.call-update
  80.3 32.5 %all-to-all-done.1 = bf16[16,1,16,2,1536]{4,2,3,1,0:T(8,128)(2,1)} async-done(((bf16[16,1,16,2,1536]{4,2,3,1,0:T(8,128)(2,1)}), bf16[16,1,16,2,1536]{4,2,3,1,0:T(8,128)(2,1)}, u32[]{:S(2)}, u32[]{:S(2)}) %all-to-all-start.1) | async-done | bytes 1572896 | tf_op jit(solution)/shard_map/all_to_all | solution.py:18
  112.8 3.3 %reshape_reshape.6 = bf16[16,16,1,2,8,192]{5,4,1,3,0,2:T(8,128)(2,1)S(1)} reshape(bf16[16,1,16,2,1536]{4,2,3,1,0:T(8,128)(2,1)} %all-to-all-done.1) | data formatting | bytes 3145728 | tf_op jit(solution)/shard_map/reshape;reshape | solution.py:122
  116.1 1.5 fusion.78
  117.6 24.0 %all-gather.3.cloned.1.call-done = bf16[256,1,2,2,768]{4,3,2,1,0:T(2,128)(2,1)} async-done(((bf16[16,1,2,2,768]{4,3,2,1,0:T(2,128)(2,1)}), bf16[256,1,2,2,768]{4,3,2,1,0:T(2,128)(2,1)}) %all-gather.3.cloned.1.call-update) | async-done | bytes 1572880 | tf_op jit(solution)/shard_map/all_gather | solution.py:118
  141.6 1.6 copy.48
  143.2 0.0 copy-start.4
  143.2 4.3 %fusion.37 = f32[8,192,2,768,1]{3,1,4,2,0:T(8,128)S(1)} fusion(bf16[16,16,1,1,8,192]{5,4,1,3,0,2:T(8,128)(2,1)} %get-tuple-element.8, bf16[16,16,1,2,2,768]{5,1,0,4,3,2:T(8,128)(2,1)S(1)} %bitcast.195), kind=kOutput, calls=%fused_computation.50 | convolution fusion | flops 1207959552 | bytes 11010048 | tf_op jit(solution)/shard_map/abesp,baemq->smqp/dot_general | solution.py:50
  147.6 6.3 %fusion.36 = f32[8,192,2,768,1]{3,1,4,2,0:T(8,128)} fusion(bf16[16,16,1,1,8,192]{5,4,1,3,0,2:T(8,128)(2,1)S(1)} %copy-done.4, bf16[16,16,1,2,2,768]{5,1,0,4,3,2:T(8,128)(2,1)S(1)} %bitcast.196), kind=kOutput, calls=%fused_computation.49 | convolution fusion | flops 1207959552 | bytes 11272192 | tf_op jit(solution)/shard_map/abesp,baemq->smqp/dot_general | solution.py:50
  153.9 0.0 copy-done.2
  153.9 2.7 %fusion.3 = f32[2,8,192,768]{3,2,0,1:T(8,128)S(1)} fusion(f32[8,192,2,768,1]{3,1,4,2,0:T(8,128)S(1)} %fusion.37, bf16[16,16,1,1,8,192]{5,4,1,3,0,2:T(8,128)(2,1)S(1)} %copy-done.3, bf16[16,16,1,2,2,768]{5,1,0,4,3,2:T(8,128)(2,1)S(1)} %bitcast.197), kind=kOutput, calls=%fused_computation.8 | convolution fusion | flops 1210318848 | bytes 20709376 | tf_op jit(solution)/shard_map/abesp,baemq->smqp/dot_general | solution.py:50
  156.6 0.8 copy.50
  157.4 10.6 %fusion.2 = f32[2,8,192,768]{3,2,0,1:T(8,128)} fusion(f32[8,192,2,768,1]{3,1,4,2,0:T(8,128)} %fusion.36, bf16[16,16,1,1,8,192]{5,4,1,3,0,2:T(8,128)(2,1)} %get-tuple-element.7, bf16[16,16,1,2,2,768]{5,1,0,4,3,2:T(8,128)(2,1)} %bitcast.198), kind=kOutput, calls=%fused_computation.6 | convolution fusion | flops 1210318848 | bytes 20709376 | tf_op jit(solution)/shard_map/abesp,baemq->smqp/dot_general | solution.py:50
  168.0 4.6 %copy.51 = f32[2,8,192,768]{3,2,1,0:T(8,128)S(1)} copy(f32[2,8,192,768]{3,2,0,1:T(8,128)} %fusion.2) | data formatting | bytes 18874368 | tf_op jit(solution)/shard_map/sub | solution.py:85
  172.6 7.1 %pad_maximum_fusion = f32[16,2,192,768]{3,2,0,1:T(8,128)} fusion(f32[16,1,192,768]{3,2,0,1:T(8,128)S(1)} %bitcast.194, f32[16,1,192,768]{3,2,0,1:T(8,128)S(1)} %bitcast.193), kind=kLoop, calls=%fused_computation.1 | loop fusion | flops 4718592 | bytes 37748736 | tf_op jit(solution)/shard_map/stack | solution.py:86
  179.7 13.0 %gather_fusion = f32[9,2,192,768]{3,2,1,0:T(8,128)} fusion(f32[16,2,192,768]{3,2,0,1:T(8,128)} %pad_maximum_fusion, s32[1024]{0:T(1024)S(1)} %pad_clamp_fusion), kind=kCustom, calls=%fused_computation | custom fusion | bytes 21233700 | tf_op jit(solution)/shard_map/jit(_take)/gather | solution.py:125
  192.8 9.8 %fusion.1 = f32[1,1,9,2,192,768]{5,4,3,2,1,0:T(8,128)} fusion(f32[9,2,192,768]{3,2,1,0:T(8,128)} %gather_fusion, pred[9]{0:T(512)(128)(4,1)S(1)} %get-tuple-element.5, pred[9]{0:T(512)(128)(4,1)S(1)} %get-tuple-element.26), kind=kLoop, calls=%fused_computation.4 | loop fusion | flops 7962624 | bytes 21233682 | tf_op jit(solution)/shard_map/mul | solution.py:127
  (23 shorter events, 0.3 us)
Async XLA Ops:
  6.5 25.1 %copy-start = (bf16[1,2,512,256]{3,2,1,0:T(8,128)(2,1)S(1)}, bf16[1,2,512,256]{3,2,1,0:T(8,128)(2,1)}, u32[]{:S(2)}) copy-start(bf16[1,2,512,256]{3,2,1,0:T(8,128)(2,1)} %param.3) | copy-start | bytes 1572868
  29.5 5.5 %copy-start.5 = (bf16[1,96,512]{2,1,0:T(8,128)(2,1)S(1)}, bf16[1,96,512]{2,1,0:T(8,128)(2,1)}, u32[]{:S(2)}) copy-start(bf16[1,96,512]{2,1,0:T(8,128)(2,1)} %get-tuple-element.11) | copy-start | bytes 294916
  29.5 5.5 %copy-start.6 = (bf16[1,96,512]{2,1,0:T(8,128)(2,1)S(1)}, bf16[1,96,512]{2,1,0:T(8,128)(2,1)}, u32[]{:S(2)}) copy-start(bf16[1,96,512]{2,1,0:T(8,128)(2,1)} %get-tuple-element.12) | copy-start | bytes 294916
  29.5 5.5 %copy-start.7 = (bf16[1,96,512]{2,1,0:T(8,128)(2,1)S(1)}, bf16[1,96,512]{2,1,0:T(8,128)(2,1)}, u32[]{:S(2)}) copy-start(bf16[1,96,512]{2,1,0:T(8,128)(2,1)} %get-tuple-element.13) | copy-start | bytes 294916
  31.6 3.5 %copy-start.8 = (bf16[1,2,256,256]{2,3,1,0:T(8,128)(2,1)S(1)}, bf16[1,2,256,256]{2,3,1,0:T(8,128)(2,1)}, u32[]{:S(2)}) copy-start(bf16[1,2,256,256]{2,3,1,0:T(8,128)(2,1)} %get-tuple-element.20) | copy-start | bytes 786436
  31.6 48.6 %copy-start.9 = (s32[1,1,9,2]{2,3,1,0:T(2,128)S(1)}, s32[1,1,9,2]{2,3,1,0:T(2,128)}, u32[]{:S(2)}) copy-start(s32[1,1,9,2]{2,3,1,0:T(2,128)} %param.5) | copy-start | bytes 220
  37.9 22.2 %all-to-all-start = ((bf16[16,1,2,1536]{3,2,1,0:T(2,128)(2,1)}), bf16[16,1,2,1536]{3,2,1,0:T(2,128)(2,1)S(1)}, u32[]{:S(2)}, u32[]{:S(2)}) async-start(bf16[16,1,2,1536]{3,2,1,0:T(2,128)(2,1)} %copy.42), calls=%async_computation | async-start | bytes 196608 | tf_op jit(solution)/shard_map/all_to_all | solution.py:117
  60.1 13.5 %all-to-all-start.2 = ((bf16[16,1,2,2,768]{4,2,3,1,0:T(2,128)(2,1)}), bf16[16,1,2,2,768]{4,2,3,1,0:T(2,128)(2,1)S(1)}, u32[]{:S(2)}, u32[]{:S(2)}) async-start(bf16[16,1,2,2,768]{4,2,3,1,0:T(2,128)(2,1)} %maximum_bitcast_fusion.7), calls=%async_computation.2 | async-start | bytes 196608 | tf_op jit(solution)/shard_map/all_to_all | solution.py:112
  75.0 37.8 %all-to-all-start.1 = ((bf16[16,1,16,2,1536]{4,2,3,1,0:T(8,128)(2,1)}), bf16[16,1,16,2,1536]{4,2,3,1,0:T(8,128)(2,1)}, u32[]{:S(2)}, u32[]{:S(2)}) async-start(bf16[16,1,16,2,1536]{4,2,3,1,0:T(8,128)(2,1)} %broadcast_in_dim.24), calls=%async_computation.1 | async-start | bytes 3145728 | tf_op jit(solution)/shard_map/all_to_all | solution.py:18
  79.4 62.2 %all-gather.3.cloned.1.call-start = ((), (), s32[]{:S(2)}) async-start(), calls=%async_computation.3 | async-start | bytes 1671168 | tf_op jit(solution)/shard_map/all_gather | solution.py:118
  143.2 10.7 %copy-start.2 = (bf16[256,1,2,2,768]{4,0,3,2,1:T(8,128)(2,1)}, bf16[256,1,2,2,768]{4,0,3,2,1:T(8,128)(2,1)S(1)}, u32[]{:S(2)}) copy-start(bf16[256,1,2,2,768]{4,0,3,2,1:T(8,128)(2,1)S(1)} %copy.48) | copy-start | bytes 4718596
  143.2 4.3 %copy-start.4 = (bf16[16,16,1,1,8,192]{5,4,1,3,0,2:T(8,128)(2,1)S(1)}, bf16[16,16,1,1,8,192]{5,4,1,3,0,2:T(8,128)(2,1)}, u32[]{:S(2)}) copy-start(bf16[16,16,1,1,8,192]{5,4,1,3,0,2:T(8,128)(2,1)} %get-tuple-element.8) | copy-start | bytes 2359300
  147.6 6.4 %copy-start.3 = (bf16[16,16,1,1,8,192]{5,4,1,3,0,2:T(8,128)(2,1)S(1)}, bf16[16,16,1,1,8,192]{5,4,1,3,0,2:T(8,128)(2,1)}, u32[]{:S(2)}) copy-start(bf16[16,16,1,1,8,192]{5,4,1,3,0,2:T(8,128)(2,1)} %get-tuple-element.7) | copy-start | bytes 2359300
  192.8 9.8 %copy-start.1 = (bf16[1,2,512,256]{3,2,1,0:T(8,128)(2,1)S(1)}, bf16[1,2,512,256]{3,2,1,0:T(8,128)(2,1)}, u32[]{:S(2)}) copy-start(bf16[1,2,512,256]{3,2,1,0:T(8,128)(2,1)} %param.3) | copy-start | bytes 1572868
Sparse Core Ops, SparseCore 0:
  83.0 58.5 all-gather.2
where the time goes:
time: 210 us; the launch traced here: 209 us
  waiting for transfers between devices  72.9 us (35%)
  other arithmetic  38.2 us (18%)
  local copies, waits for them, and re-layouts  33.1 us (16%)
  matrix products  28.7 us (14%)
  starting transfers between devices  22.9 us (11%)
  between operations  13.7 us (7%)
    all_to_all x1, waiting for transfers between devices, copy_for_each(): lax.all_to_all(jnp.broadcast_to(x[None], (length, *x.shape)), axis, 0, 0,...  32.5 us
    dot_general x6, matrix products, contract(): jnp.einsum(formula, left_side, right_side, preferred_element_type=jnp.flo...  28.7 us
    all_gather x1, waiting for transfers between devices, body(): row_panel = lax.all_gather(row_mine, ('elec', 'col'), axis=0, tiled=True)  24 us
    gather x1, local copies, waits for them, and re-layouts, body(): result = jnp.take(flat_blocks, upper_pick * spread + column, axis=0)  13 us
    another operation x5, other arithmetic  12.8 us
    all_to_all x1, starting transfers between devices, body(): lax.all_to_all(col_send, ('elec', 'col'), split_axis=0, concat_axis=1, ti...  12.4 us
    mul x1, other arithmetic, body(): result = result * (1.0 / math.sqrt(total_electrons))  9.79 us
    all_to_all x1, waiting for transfers between devices, body(): lax.all_to_all(col_send, ('elec', 'col'), split_axis=0, concat_axis=1, ti...  8.81 us
  transfers between devices with their start and end apart: 4, of which 4 were waited for; matrix products, arithmetic and copies ran while one was open for 3% of the time, Pallas kernels for 0%

commit v1 on v0

--- a/solution.py
+++ b/solution.py
@@ -115,7 +115,12 @@
         group_size, electrons, 2, spread * quarter
     )
     col_mine = lax.all_to_all(col_send, ("elec", "col"), split_axis=0, concat_axis=1, tiled=True)
-    row_panel = lax.all_gather(row_mine, ("elec", "col"), axis=0, tiled=True)
+    row_panel = jnp.concatenate(
+        lax.all_to_all(
+            jnp.stack([row_mine] * lax.axis_size(("elec", "col"))), ("elec", "col"), 0, 0
+        ),
+        axis=0,
+    )
     row_panel = row_panel.reshape(group_size, row_devices, electrons, 2, 2, TILE)
     shard_piece = gathered_copies(col_mine, "row", 0)
     piece_rows = shard_piece.shape[0]

time: 210 us -> 218 us (1.038)
  the two profiles are of different devices: /device:TPU:1 before, /device:TPU:32 now
where the time goes in v1:
time: 218 us
  waiting for transfers between devices  89.5 us (41%)
  other arithmetic  38.2 us (18%)
  local copies, waits for them, and re-layouts  33.8 us (16%)
  matrix products  28.7 us (13%)
  starting transfers between devices  27.2 us (12%)
    all_to_all x1, waiting for transfers between devices, body(): lax.all_to_all(jnp.stack([row_mine] * lax.axis_size(('elec', 'col'))), ('...  37.6 us
    all_to_all x1, waiting for transfers between devices, copy_for_each(): lax.all_to_all(jnp.broadcast_to(x[None], (length, *x.shape)), axis, 0, 0,...  36.1 us
    dot_general x6, matrix products, contract(): jnp.einsum(formula, left_side, right_side, preferred_element_type=jnp.flo...  28.7 us
    gather x1, local copies, waits for them, and re-layouts, body(): result = jnp.take(flat_blocks, upper_pick * spread + column, axis=0)  13 us
    another operation x5, other arithmetic  12.8 us
    all_to_all x1, starting transfers between devices, body(): lax.all_to_all(col_send, ('elec', 'col'), split_axis=0, concat_axis=1, ti...  10.1 us
    mul x1, other arithmetic, body(): result = result * (1.0 / math.sqrt(total_electrons))  9.79 us
    all_to_all x1, waiting for transfers between devices, body(): lax.all_to_all(col_send, ('elec', 'col'), split_axis=0, concat_axis=1, ti...  9.09 us
  transfers between devices with their start and end apart: 4, of which 4 were waited for; matrix products, arithmetic and copies ran while one was open for 3% of the time, Pallas kernels for 0%

profile of v1, /device:TPU:32, one launch (start us, length us, event | category | flops | bytes accessed | tf_op | source)
XLA Modules:
  0.0 217.6 jit_solution(13212263712704413773)
XLA Ops:
  0.0 0.0 copy-start
  0.0 1.0 negate_convert_fusion.1
  1.0 1.7 multiply_convert_fusion.1
  2.7 1.7 multiply_convert_fusion.3
  4.4 4.4 %negate_convert_fusion = (bf16[1,512,512]{2,1,0:T(8,128)(2,1)S(1)}, bf16[1,512,512]{2,1,0:T(8,128)(2,1)S(1)}) fusion(), kind=kLoop, calls=%fused_computation.42 | loop fusion | flops 4980736 | bytes 1048576 | tf_op jit(solution)/shard_map/convert.21
  8.8 4.0 %fusion.35 = bf16[1,512,512]{2,1,0:T(8,128)(2,1)S(1)} fusion(), kind=kLoop, calls=%fused_computation.49 | loop fusion | flops 4194304 | bytes 524288 | tf_op jit(solution)/shard_map/convert.17
  12.8 1.5 fusion.28
  14.3 2.1 copy.22
  16.3 2.8 %fusion.79 = (f32[512,256]{0,1:T(8,128)S(1)}, f32[512,256]{0,1:T(8,128)S(1)}) fusion(f32[512,256]{0,1:T(8,128)} %copy.22), kind=kLoop, calls=%fused_computation.119 | loop fusion | bytes 1572864 | tf_op jit(solution)/shard_map/sin | solution.py:57
  19.1 2.4 %fusion.72 = (bf16[1,96,512]{2,1,0:T(8,128)(2,1)}, bf16[1,96,512]{2,1,0:T(8,128)(2,1)}, bf16[1,96,512]{2,1,0:T(8,128)(2,1)}) fusion(f32[512,512]{1,0:T(8,128)} %fusion.28), kind=kLoop, calls=%fused_computation.105 | loop fusion | flops 294912 | bytes 491520 | tf_op jit(solution)/shard_map/stack | solution.py:38
  21.5 1.5 maximum_bitcast_fusion
  23.0 2.0 fusion.59
  25.1 0.0 copy-done
  25.1 3.2 %convolution_bitcast_fusion = f32[1,2,512,256]{2,3,1,0:T(8,128)S(1)} fusion(bf16[1,2,512,512]{3,2,1,0:T(8,128)(2,1)} %get-tuple-element.17, bf16[1,2,512,512]{3,2,1,0:T(8,128)(2,1)} %get-tuple-element.16, bf16[1,2,256,256]{2,3,0,1:T(8,128)(2,1)} %get-tuple-element.19, bf16[1,2,256,256]{2,3,0,1:T(8,128)(2,1)} %get-tuple-element.18, ...), kind=kOutput, calls=%fused_computation.21 | convolution fusion | flops 806879232 | bytes 4194304 | tf_op jit(solution)/shard_map/ecxy,cdyz->edxz/dot_general | solution.py:50
  28.2 0.0 copy-start.10
  28.2 0.3 fusion.63
  28.5 0.0 copy-done.6
  28.5 0.0 copy-done.7
  28.6 1.7 fusion.22
  30.3 0.1 reshape_reshape_reshape.3
  30.5 0.1 reshape.303
  30.6 0.7 copy.27
  31.4 10.1 %all-to-all-start = ((bf16[16,1,2,1536]{3,2,1,0:T(2,128)(2,1)}), bf16[16,1,2,1536]{3,2,1,0:T(2,128)(2,1)S(1)}, u32[]{:S(2)}, u32[]{:S(2)}) async-start(bf16[16,1,2,1536]{3,2,1,0:T(2,128)(2,1)} %copy.27), calls=%async_computation | async-start | bytes 196608 | tf_op jit(solution)/shard_map/all_to_all | solution.py:117
  41.5 0.1 reshape_reshape.10
  41.7 0.8 maximum_bitcast_fusion.7
  42.5 9.1 %all-to-all-done = bf16[16,1,2,1536]{3,2,1,0:T(2,128)(2,1)S(1)} async-done(((bf16[16,1,2,1536]{3,2,1,0:T(2,128)(2,1)}), bf16[16,1,2,1536]{3,2,1,0:T(2,128)(2,1)S(1)}, u32[]{:S(2)}, u32[]{:S(2)}) %all-to-all-start) | async-done | bytes 98336 | tf_op jit(solution)/shard_map/all_to_all | solution.py:117
  51.6 6.9 %all-to-all-start.2 = ((bf16[16,1,2,2,768]{4,2,3,1,0:T(2,128)(2,1)}), bf16[16,1,2,2,768]{4,2,3,1,0:T(2,128)(2,1)S(1)}, u32[]{:S(2)}, u32[]{:S(2)}) async-start(bf16[16,1,2,2,768]{4,2,3,1,0:T(2,128)(2,1)} %maximum_bitcast_fusion.7), calls=%async_computation.2 | async-start | bytes 196608 | tf_op jit(solution)/shard_map/all_to_all | solution.py:112
  58.6 6.7 %all-to-all-done.2 = bf16[16,1,2,2,768]{4,2,3,1,0:T(2,128)(2,1)S(1)} async-done(((bf16[16,1,2,2,768]{4,2,3,1,0:T(2,128)(2,1)}), bf16[16,1,2,2,768]{4,2,3,1,0:T(2,128)(2,1)S(1)}, u32[]{:S(2)}, u32[]{:S(2)}) %all-to-all-start.2) | async-done | bytes 98336 | tf_op jit(solution)/shard_map/all_to_all | solution.py:112
  65.3 1.3 broadcast_in_dim.24
  66.6 5.5 %all-to-all-start.1 = ((bf16[16,1,16,2,1536]{4,2,3,1,0:T(8,128)(2,1)}), bf16[16,1,16,2,1536]{4,2,3,1,0:T(8,128)(2,1)S(1)}, u32[]{:S(2)}, u32[]{:S(2)}) async-start(bf16[16,1,16,2,1536]{4,2,3,1,0:T(8,128)(2,1)} %broadcast_in_dim.24), calls=%async_computation.1 | async-start | bytes 3145728 | tf_op jit(solution)/shard_map/all_to_all | solution.py:18
  72.2 36.1 %all-to-all-done.1 = bf16[16,1,16,2,1536]{4,2,3,1,0:T(8,128)(2,1)S(1)} async-done(((bf16[16,1,16,2,1536]{4,2,3,1,0:T(8,128)(2,1)}), bf16[16,1,16,2,1536]{4,2,3,1,0:T(8,128)(2,1)S(1)}, u32[]{:S(2)}, u32[]{:S(2)}) %all-to-all-start.1) | async-done | bytes 1572896 | tf_op jit(solution)/shard_map/all_to_all | solution.py:18
  108.3 1.5 stack.184
  109.7 4.6 %all-to-all-start.3 = ((bf16[16,1,16,2,2,768]{5,2,4,3,1,0:T(8,128)(2,1)}), bf16[16,1,16,2,2,768]{5,2,4,3,1,0:T(8,128)(2,1)}, u32[]{:S(2)}, u32[]{:S(2)}) async-start(bf16[16,1,16,2,2,768]{5,2,4,3,1,0:T(8,128)(2,1)} %stack.184), calls=%async_computation.3 | async-start | bytes 3145728 | tf_op jit(solution)/shard_map/all_to_all | solution.py:119
  114.4 3.3 %reshape_reshape.9 = bf16[16,16,1,2,8,192]{5,4,1,3,0,2:T(8,128)(2,1)S(1)} reshape(bf16[16,1,16,2,1536]{4,2,3,1,0:T(8,128)(2,1)} %copy-done.2) | data formatting | bytes 3145728 | tf_op jit(solution)/shard_map/reshape;reshape | solution.py:127
  117.7 1.5 fusion.78
  119.2 37.6 %all-to-all-done.3 = bf16[16,1,16,2,2,768]{5,2,4,3,1,0:T(8,128)(2,1)} async-done(((bf16[16,1,16,2,2,768]{5,2,4,3,1,0:T(8,128)(2,1)}), bf16[16,1,16,2,2,768]{5,2,4,3,1,0:T(8,128)(2,1)}, u32[]{:S(2)}, u32[]{:S(2)}) %all-to-all-start.3) | async-done | bytes 1572896 | tf_op jit(solution)/shard_map/all_to_all | solution.py:119
  156.8 1.5 copy.63
  158.3 0.0 copy-start.5
  158.3 4.3 %fusion.37 = f32[8,192,2,768,1]{3,1,4,2,0:T(8,128)S(1)} fusion(bf16[16,16,1,1,8,192]{5,4,1,3,0,2:T(8,128)(2,1)} %get-tuple-element.8, bf16[16,16,1,2,2,768]{5,1,0,4,3,2:T(8,128)(2,1)S(1)} %bitcast.198), kind=kOutput, calls=%fused_computation.51 | convolution fusion | flops 1207959552 | bytes 11010048 | tf_op jit(solution)/shard_map/abesp,baemq->smqp/dot_general | solution.py:50
  162.7 6.3 %fusion.36 = f32[8,192,2,768,1]{3,1,4,2,0:T(8,128)} fusion(bf16[16,16,1,1,8,192]{5,4,1,3,0,2:T(8,128)(2,1)S(1)} %copy-done.5, bf16[16,16,1,2,2,768]{5,1,0,4,3,2:T(8,128)(2,1)S(1)} %bitcast.199), kind=kOutput, calls=%fused_computation.50 | convolution fusion | flops 1207959552 | bytes 11272192 | tf_op jit(solution)/shard_map/abesp,baemq->smqp/dot_general | solution.py:50
  169.0 2.7 %fusion.3 = f32[2,8,192,768]{3,2,0,1:T(8,128)S(1)} fusion(f32[8,192,2,768,1]{3,1,4,2,0:T(8,128)S(1)} %fusion.37, bf16[16,16,1,1,8,192]{5,4,1,3,0,2:T(8,128)(2,1)S(1)} %copy-done.4, bf16[16,16,1,2,2,768]{5,1,0,4,3,2:T(8,128)(2,1)S(1)} %bitcast.200), kind=kOutput, calls=%fused_computation.8 | convolution fusion | flops 1210318848 | bytes 20709376 | tf_op jit(solution)/shard_map/abesp,baemq->smqp/dot_general | solution.py:50
  171.7 0.8 copy.35
  172.5 10.6 %fusion.2 = f32[2,8,192,768]{3,2,0,1:T(8,128)} fusion(f32[8,192,2,768,1]{3,1,4,2,0:T(8,128)} %fusion.36, bf16[16,16,1,1,8,192]{5,4,1,3,0,2:T(8,128)(2,1)} %get-tuple-element.7, bf16[16,16,1,2,2,768]{5,1,0,4,3,2:T(8,128)(2,1)} %bitcast.201), kind=kOutput, calls=%fused_computation.6 | convolution fusion | flops 1210318848 | bytes 20709376 | tf_op jit(solution)/shard_map/abesp,baemq->smqp/dot_general | solution.py:50
  183.1 4.6 %copy.36 = f32[2,8,192,768]{3,2,1,0:T(8,128)S(1)} copy(f32[2,8,192,768]{3,2,0,1:T(8,128)} %fusion.2) | data formatting | bytes 18874368 | tf_op jit(solution)/shard_map/sub | solution.py:85
  187.7 7.1 %pad_maximum_fusion = f32[16,2,192,768]{3,2,0,1:T(8,128)} fusion(f32[16,1,192,768]{3,2,0,1:T(8,128)S(1)} %bitcast.197, f32[16,1,192,768]{3,2,0,1:T(8,128)S(1)} %bitcast.196), kind=kLoop, calls=%fused_computation.1 | loop fusion | flops 4718592 | bytes 37748736 | tf_op jit(solution)/shard_map/stack | solution.py:86
  194.8 13.0 %gather_fusion = f32[9,2,192,768]{3,2,1,0:T(8,128)} fusion(f32[16,2,192,768]{3,2,0,1:T(8,128)} %pad_maximum_fusion, s32[1024]{0:T(1024)S(1)} %pad_clamp_fusion), kind=kCustom, calls=%fused_computation | custom fusion | bytes 21233700 | tf_op jit(solution)/shard_map/jit(_take)/gather | solution.py:130
  207.9 9.8 %fusion.1 = f32[1,1,9,2,192,768]{5,4,3,2,1,0:T(8,128)} fusion(f32[9,2,192,768]{3,2,1,0:T(8,128)} %gather_fusion, pred[9]{0:T(512)(128)(4,1)S(1)} %get-tuple-element.5, pred[9]{0:T(512)(128)(4,1)S(1)} %get-tuple-element.26), kind=kLoop, calls=%fused_computation.4 | loop fusion | flops 7962624 | bytes 21233682 | tf_op jit(solution)/shard_map/mul | solution.py:132
  217.6 0.0 copy-done.1
  (25 shorter events, 0.3 us)
Async XLA Ops:
  0.0 25.1 %copy-start = (bf16[1,2,512,256]{3,2,1,0:T(8,128)(2,1)S(1)}, bf16[1,2,512,256]{3,2,1,0:T(8,128)(2,1)}, u32[]{:S(2)}) copy-start(bf16[1,2,512,256]{3,2,1,0:T(8,128)(2,1)} %param.3) | copy-start | bytes 1572868
  23.0 5.5 %copy-start.6 = (bf16[1,96,512]{2,1,0:T(8,128)(2,1)S(1)}, bf16[1,96,512]{2,1,0:T(8,128)(2,1)}, u32[]{:S(2)}) copy-start(bf16[1,96,512]{2,1,0:T(8,128)(2,1)} %get-tuple-element.11) | copy-start | bytes 294916
  23.0 5.5 %copy-start.7 = (bf16[1,96,512]{2,1,0:T(8,128)(2,1)S(1)}, bf16[1,96,512]{2,1,0:T(8,128)(2,1)}, u32[]{:S(2)}) copy-start(bf16[1,96,512]{2,1,0:T(8,128)(2,1)} %get-tuple-element.12) | copy-start | bytes 294916
  23.0 5.5 %copy-start.8 = (bf16[1,96,512]{2,1,0:T(8,128)(2,1)S(1)}, bf16[1,96,512]{2,1,0:T(8,128)(2,1)}, u32[]{:S(2)}) copy-start(bf16[1,96,512]{2,1,0:T(8,128)(2,1)} %get-tuple-element.13) | copy-start | bytes 294916
  25.1 3.5 %copy-start.9 = (bf16[1,2,256,256]{2,3,1,0:T(8,128)(2,1)S(1)}, bf16[1,2,256,256]{2,3,1,0:T(8,128)(2,1)}, u32[]{:S(2)}) copy-start(bf16[1,2,256,256]{2,3,1,0:T(8,128)(2,1)} %get-tuple-element.20) | copy-start | bytes 786436
  28.2 86.1 %copy-start.10 = (s32[1,1,9,2]{2,3,1,0:T(2,128)S(1)}, s32[1,1,9,2]{2,3,1,0:T(2,128)}, u32[]{:S(2)}) copy-start(s32[1,1,9,2]{2,3,1,0:T(2,128)} %param.5) | copy-start | bytes 220
  31.4 20.2 %all-to-all-start = ((bf16[16,1,2,1536]{3,2,1,0:T(2,128)(2,1)}), bf16[16,1,2,1536]{3,2,1,0:T(2,128)(2,1)S(1)}, u32[]{:S(2)}, u32[]{:S(2)}) async-start(bf16[16,1,2,1536]{3,2,1,0:T(2,128)(2,1)} %copy.27), calls=%async_computation | async-start | bytes 196608 | tf_op jit(solution)/shard_map/all_to_all | solution.py:117
  51.6 13.7 %all-to-all-start.2 = ((bf16[16,1,2,2,768]{4,2,3,1,0:T(2,128)(2,1)}), bf16[16,1,2,2,768]{4,2,3,1,0:T(2,128)(2,1)S(1)}, u32[]{:S(2)}, u32[]{:S(2)}) async-start(bf16[16,1,2,2,768]{4,2,3,1,0:T(2,128)(2,1)} %maximum_bitcast_fusion.7), calls=%async_computation.2 | async-start | bytes 196608 | tf_op jit(solution)/shard_map/all_to_all | solution.py:112
  66.6 41.7 %all-to-all-start.1 = ((bf16[16,1,16,2,1536]{4,2,3,1,0:T(8,128)(2,1)}), bf16[16,1,16,2,1536]{4,2,3,1,0:T(8,128)(2,1)S(1)}, u32[]{:S(2)}, u32[]{:S(2)}) async-start(bf16[16,1,16,2,1536]{4,2,3,1,0:T(8,128)(2,1)} %broadcast_in_dim.24), calls=%async_computation.1 | async-start | bytes 3145728 | tf_op jit(solution)/shard_map/all_to_all | solution.py:18
  108.3 6.1 %copy-start.2 = (bf16[16,1,16,2,1536]{4,2,3,1,0:T(8,128)(2,1)}, bf16[16,1,16,2,1536]{4,2,3,1,0:T(8,128)(2,1)S(1)}, u32[]{:S(2)}) copy-start(bf16[16,1,16,2,1536]{4,2,3,1,0:T(8,128)(2,1)S(1)} %all-to-all-done.1) | copy-start | bytes 4718596
  109.7 47.0 %all-to-all-start.3 = ((bf16[16,1,16,2,2,768]{5,2,4,3,1,0:T(8,128)(2,1)}), bf16[16,1,16,2,2,768]{5,2,4,3,1,0:T(8,128)(2,1)}, u32[]{:S(2)}, u32[]{:S(2)}) async-start(bf16[16,1,16,2,2,768]{5,2,4,3,1,0:T(8,128)(2,1)} %stack.184), calls=%async_computation.3 | async-start | bytes 3145728 | tf_op jit(solution)/shard_map/all_to_all | solution.py:119
  158.3 10.7 %copy-start.3 = (bf16[16,1,16,2,2,768]{5,2,0,4,3,1:T(8,128)(2,1)}, bf16[16,1,16,2,2,768]{5,2,0,4,3,1:T(8,128)(2,1)S(1)}, u32[]{:S(2)}) copy-start(bf16[16,1,16,2,2,768]{5,2,0,4,3,1:T(8,128)(2,1)S(1)} %copy.63) | copy-start | bytes 4718596
  158.3 4.3 %copy-start.5 = (bf16[16,16,1,1,8,192]{5,4,1,3,0,2:T(8,128)(2,1)S(1)}, bf16[16,16,1,1,8,192]{5,4,1,3,0,2:T(8,128)(2,1)}, u32[]{:S(2)}) copy-start(bf16[16,16,1,1,8,192]{5,4,1,3,0,2:T(8,128)(2,1)} %get-tuple-element.8) | copy-start | bytes 2359300
  162.7 6.4 %copy-start.4 = (bf16[16,16,1,1,8,192]{5,4,1,3,0,2:T(8,128)(2,1)S(1)}, bf16[16,16,1,1,8,192]{5,4,1,3,0,2:T(8,128)(2,1)}, u32[]{:S(2)}) copy-start(bf16[16,16,1,1,8,192]{5,4,1,3,0,2:T(8,128)(2,1)} %get-tuple-element.7) | copy-start | bytes 2359300
  207.9 9.8 %copy-start.1 = (bf16[1,2,512,256]{3,2,1,0:T(8,128)(2,1)S(1)}, bf16[1,2,512,256]{3,2,1,0:T(8,128)(2,1)}, u32[]{:S(2)}) copy-start(bf16[1,2,512,256]{3,2,1,0:T(8,128)(2,1)} %param.3) | copy-start | bytes 1572868
